TPU v7x, 512 devices: a whole 4x8x8 slice. The times are simulated.
512 devices in a mesh: tp: 64 (over y, z_hi, core), ep: 8 (over x, z_lo).
Axes of the slice: x: 4, y: 8, z: 8 (z_hi: 4, z_lo: 2; z = z_hi * 2 + z_lo), core: 2. Of those that a mesh axis runs over, the one named last changes fastest.
Arguments:
- residual: bfloat16 [8, 7168, 256], P('ep', 'tp')
- out_grad: bfloat16 [8, 7168, 256], P('ep', 'tp'), may hold values from -6 to 6
- norm_gain: float32 [7168], P('tp'), may hold values from 0.25 to 1.75
- context: bfloat16 [8, 16384, 256], P('ep', 'tp'), may hold values from -0.3125 to 0.3125
- w_out: bfloat16 [7168, 16384], P('ep', 'tp'), may hold values from -0.046875 to 0.046875
- w_gate: bfloat16 [8, 7168, 2048], P('ep', 'tp'), may hold values from -0.0625 to 0.0625
- w_up: bfloat16 [8, 7168, 2048], P('ep', 'tp'), may hold values from -0.0625 to 0.0625
- w_down: bfloat16 [8, 7168, 2048], P('ep', 'tp'), may hold values from -0.125 to 0.125
- slot_token: int32 [8, 8, 8], P('ep'), may hold values from 0 to 255, as said below
- slot_count: int32 [8, 8], P('ep'), may hold values from 1 to 8, as said below
- slot_gate: float32 [8, 8, 8], P('ep'), may hold values from 0.25 to 2.5
Outputs:
- resid_grad: bfloat16 [8, 7168, 256], P('ep', 'tp')
- context_grad: bfloat16 [8, 16384, 256], P('ep', 'tp')
- w_out_grad: bfloat16 [7168, 16384], P('ep', 'tp')
- gate_grad: bfloat16 [8, 7168, 2048], P('ep', 'tp')
- up_grad: bfloat16 [8, 7168, 2048], P('ep', 'tp')
- down_grad: bfloat16 [8, 7168, 2048], P('ep', 'tp')
Inputs may be any that keep to these rules, and one draw needn't show every extreme that they name: `slot_token`: within one group and expert the 8 token positions are distinct; slots at or beyond slot_count are unused. `slot_count`: in every draw one expert has 8 tokens from every group.
All inputs are finite; a program needn't handle non-finite values.
Results may differ from a plain program's by a relative error of at most 0.014.
Values may be sent and summed in bfloat16 or wider, within the bound.
A program may use at most 64 MiB of HBM per device.

v0:
```python
import jax
import jax.numpy as jnp
from jax import lax
from jax.sharding import PartitionSpec as P

norm_eps = 1e-06


def contract_rows(left, right):
    return lax.dot_general(
        left, right, (((0,), (0,)), ((), ())), preferred_element_type=jnp.float32
    )


def contract_cols(left, right):
    return lax.dot_general(
        left, right, (((1,), (1,)), ((), ())), preferred_element_type=jnp.float32
    )


def activate(pre_gate, pre_up, hid_grad):
    sigmoid_gate = jax.nn.sigmoid(pre_gate)
    silu_gate = pre_gate * sigmoid_gate
    hidden = (silu_gate * pre_up).astype(jnp.bfloat16)
    d_gate = (hid_grad * pre_up * sigmoid_gate * (1.0 + pre_gate * (1.0 - sigmoid_gate))).astype(
        jnp.bfloat16
    )
    d_up = (hid_grad * silu_gate).astype(jnp.bfloat16)
    return (hidden, d_gate, d_up)


def shards(
    residual,
    out_grad,
    norm_gain,
    context,
    w_out,
    w_gate,
    w_up,
    w_down,
    slot_token,
    slot_count,
    slot_gate,
):
    tp_count = lax.axis_size("tp")
    stream = residual[0].astype(jnp.float32)
    grad_in = out_grad[0].astype(jnp.float32)
    feat_share, group_rows = stream.shape
    features = feat_share * tp_count
    square = lax.psum(jnp.sum(stream * stream, axis=0), "tp")
    inv_rms = lax.rsqrt(square / features + norm_eps)[None, :]
    normed = stream * inv_rms
    gain_col = norm_gain[:, None]
    inputs = (normed * gain_col).astype(jnp.bfloat16)
    slot_table = slot_token[0]
    capacity = slot_table.shape[1]
    live_mask = jnp.arange(capacity)[None, :] < slot_count[0][:, None]
    one_hot = (
        (slot_table[:, :, None] == jnp.arange(group_rows)[None, None, :]) & live_mask[:, :, None]
    ).astype(jnp.bfloat16)
    send_x = jnp.einsum("dt,ect->edc", inputs, one_hot, preferred_element_type=jnp.float32).astype(
        jnp.bfloat16
    )
    go_rows = jnp.einsum("dt,ect->edc", out_grad[0], one_hot, preferred_element_type=jnp.float32)
    send_go = (slot_gate[0][:, None, :] * go_rows).astype(jnp.bfloat16)
    recv_x, recv_go = (
        lax.all_to_all(send_x, "ep", split_axis=0, concat_axis=2, tiled=True),
        lax.all_to_all(send_go, "ep", split_axis=0, concat_axis=2, tiled=True),
    )
    rows_x = recv_x[0]
    rows_go = recv_go[0]
    gate_w = w_gate[0]
    up_w = w_up[0]
    down_w = w_down[0]
    gate_part = contract_rows(rows_x, gate_w)
    up_part = contract_rows(rows_x, up_w)
    hid_part = contract_rows(rows_go, down_w)
    pre_gate, pre_up, hid_grad = lax.psum((gate_part, up_part, hid_part), "tp")
    hidden, d_gate, d_up = activate(pre_gate, pre_up, hid_grad)
    down_grad = jnp.dot(rows_go, hidden, preferred_element_type=jnp.float32).astype(jnp.bfloat16)[
        None
    ]
    gate_grad = jnp.dot(rows_x, d_gate, preferred_element_type=jnp.float32).astype(jnp.bfloat16)[
        None
    ]
    up_grad = jnp.dot(rows_x, d_up, preferred_element_type=jnp.float32).astype(jnp.bfloat16)[None]
    slot_back = (contract_cols(gate_w, d_gate) + contract_cols(up_w, d_up)).astype(jnp.bfloat16)
    returned = lax.all_to_all(slot_back[None], "ep", split_axis=2, concat_axis=0, tiled=True)
    in_grad = jnp.einsum(
        "edc,ect->dt", returned, one_hot, preferred_element_type=jnp.float32
    ).astype(jnp.bfloat16)
    scaled = in_grad.astype(jnp.float32) * gain_col
    dots = lax.psum(jnp.sum(scaled * normed, axis=0), "tp")
    resid = (grad_in + inv_rms * (scaled - normed * (dots / features)[None, :])).astype(
        jnp.bfloat16
    )
    full_grad = lax.all_gather(resid, "tp", axis=0, tiled=True)
    grad_block = lax.all_to_all(full_grad, "ep", split_axis=0, concat_axis=1, tiled=True)
    ctx_local = context[0]
    ctx_all = lax.all_gather(ctx_local, "ep", axis=1, tiled=True)
    weight_sum = contract_cols(grad_block, ctx_all)
    ctx_total = contract_rows(lax.all_gather(w_out, "ep", axis=0, tiled=True), full_grad)
    return (
        resid[None],
        ctx_total.astype(jnp.bfloat16)[None],
        weight_sum.astype(jnp.bfloat16),
        gate_grad,
        up_grad,
        down_grad,
    )


def solution(mesh):
    return jax.shard_map(
        shards,
        mesh=mesh,
        in_specs=(
            P("ep", "tp", None),
            P("ep", "tp", None),
            P("tp"),
            P("ep", "tp", None),
            P("ep", "tp"),
            P("ep", "tp", None),
            P("ep", "tp", None),
            P("ep", "tp", None),
            P("ep", None, None),
            P("ep", None),
            P("ep", None, None),
        ),
        out_specs=(
            P("ep", "tp", None),
            P("ep", "tp", None),
            P("ep", "tp"),
            P("ep", "tp", None),
            P("ep", "tp", None),
            P("ep", "tp", None),
        ),
        check_vma=False,
    )
```

profile of v0, /device:TPU:2, one launch (start us, length us, event | category | flops | bytes accessed | tf_op | source)
XLA Modules:
  0.0 1152.4 jit_solution(9309882180991946875)
XLA Ops:
  7.2 0.9 fusion.32
  8.1 150.2 %psum.35 = f32[256]{0:T(256)S(1)} all-reduce(f32[256]{0:T(256)S(1)} %fusion.32), channel_id=1, replica_groups=mesh['tp'=64,'ep'=8] {'tp'}, use_global_device_ids=true, to_apply=%region_1.0 | all-reduce | flops 256 | bytes 2048 | tf_op jit(solution)/shard_map/psum | solution.py:50
  158.3 0.7 iota_compare_fusion.1
  159.1 1.6 fusion.9
  160.7 5.7 all-to-all-start.1
  166.5 1.6 fusion.11
  168.1 3.1 all-to-all-done.1
  171.2 4.7 all-to-all-start
  175.9 1.0 fusion.16
  177.0 2.1 fusion.19
  179.1 1.7 all-to-all-done
  180.7 2.0 fusion.21
  182.8 554.5 %all-reduce.3.cloned.1.call-done = (f32[64,2048]{1,0:T(8,128)}, f32[64,2048]{1,0:T(8,128)}, f32[64,2048]{1,0:T(8,128)}) async-done(((f32[64,2048]{1,0:T(8,128)}, f32[64,2048]{1,0:T(8,128)}, f32[64,2048]{1,0:T(8,128)}), (f32[64,2048]{1,0:T(8,128)}, f32[64,2048]{1,0:T(8,128)}, f32[64,2048]{1,0:T(8,128)})) %all-reduce.3.cloned.1.call-update) | async-done | bytes 1572880 | tf_op jit(solution)/shard_map/psum | solution.py:78
  737.3 1.6 multiply_convert_fusion.1
  739.6 0.5 broadcast.36
  740.1 0.7 reduce
  740.9 9.5 all_to_all.67
  750.9 142.3 %psum.39 = f32[256]{0:T(256)S(1)} all-reduce(f32[256]{0:T(256)S(1)} %get-tuple-element.35), channel_id=1, replica_groups=mesh['tp'=64,'ep'=8] {'tp'}, use_global_device_ids=true, to_apply=%region_6.0 | all-reduce | flops 256 | bytes 2048 | tf_op jit(solution)/shard_map/psum | solution.py:93
  893.2 0.7 fusion.31
  893.9 0.7 all-gather.7.cloned.1.call-update
  894.6 78.9 %all-gather.5.cloned.1.call-done = bf16[7168,256]{1,0:T(8,128)(2,1)} async-done(((bf16[112,256]{1,0:T(8,128)(2,1)}), bf16[7168,256]{1,0:T(8,128)(2,1)}) %all-gather.5.cloned.1.call-update) | async-done | bytes 3670032 | tf_op jit(solution)/shard_map/all_gather | solution.py:97
  973.5 6.2 copy.32
  979.8 6.5 all-to-all-start.3
  986.3 0.6 all-gather.9.cloned.1.call-update
  986.9 1.1 fusion
  987.9 1.1 fusion.1
  989.0 1.1 fusion.2
  990.1 107.2 %all-gather.7.cloned.1.call-done = bf16[7168,256]{1,0:T(8,128)(2,1)} async-done(((bf16[896,256]{1,0:T(8,128)(2,1)}), bf16[7168,256]{1,0:T(8,128)(2,1)}) %all-gather.7.cloned.1.call-update) | async-done | bytes 3670032 | tf_op jit(solution)/shard_map/all_gather | solution.py:102
  1097.3 4.3 fusion.3
  1101.6 0.8 copy.33
  1102.4 39.3 %all-gather.9.cloned.1.call-done = bf16[1,256,2048]{2,1,0:T(8,128)(2,1)} async-done(((bf16[1,256,256]{2,1,0:T(8,128)(2,1)}), bf16[1,256,2048]{2,1,0:T(8,128)(2,1)}) %all-gather.9.cloned.1.call-update) | async-done | bytes 1048592 | tf_op jit(solution)/shard_map/all_gather | solution.py:100
  1141.6 4.3 convolution_convert_fusion.3
  (31 shorter events, 1.2 us)
Async XLA Ops:
  7.2 168.8 %copy-start = (bf16[1,112,2048]{2,1,0:T(8,128)(2,1)S(1)}, bf16[1,112,2048]{2,1,0:T(8,128)(2,1)}, u32[]{:S(2)}) copy-start(bf16[1,112,2048]{2,1,0:T(8,128)(2,1)} %param.16) | copy-start | bytes 1376260
  160.7 10.5 all-to-all-start.1
  171.2 9.5 all-to-all-start
  175.9 563.3 %copy-start.1 = (bf16[1,112,2048]{2,1,0:T(8,128)(2,1)S(1)}, bf16[1,112,2048]{2,1,0:T(8,128)(2,1)}, u32[]{:S(2)}) copy-start(bf16[1,112,2048]{2,1,0:T(8,128)(2,1)} %param.17) | copy-start | bytes 1376260
  175.9 561.4 %all-reduce.3.cloned.1.call-start = ((), (), s32[]{:S(2)}) async-start(), calls=%async_computation.7 | async-start | bytes 3145728 | tf_op jit(solution)/shard_map/psum | solution.py:78
  176.9 573.6 %copy-start.4 = (bf16[1,112,256]{2,1,0:T(8,128)(2,1)S(1)}, bf16[1,112,256]{2,1,0:T(8,128)(2,1)}, u32[]{:S(2)}) copy-start(bf16[1,112,256]{2,1,0:T(8,128)(2,1)} %param.11) | copy-start | bytes 172036
  176.9 573.6 %copy-start.6 = (s32[1,8,8]{2,1,0:T(8,128)S(1)}, s32[1,8,8]{2,1,0:T(8,128)}, u32[]{:S(2)}) copy-start(s32[1,8,8]{2,1,0:T(8,128)} %param.19) | copy-start | bytes 772
  177.0 573.6 %copy-start.7 = (f32[112]{0:T(128)S(1)}, f32[112]{0:T(128)}, u32[]{:S(2)}) copy-start(f32[112]{0:T(128)} %param.13) | copy-start | bytes 1348
  177.0 716.3 %copy-start.5 = (bf16[1,112,256]{2,1,0:T(8,128)(2,1)S(1)}, bf16[1,112,256]{2,1,0:T(8,128)(2,1)}, u32[]{:S(2)}) copy-start(bf16[1,112,256]{2,1,0:T(8,128)(2,1)} %param.12) | copy-start | bytes 172036
  182.8 790.7 %all-gather.5.cloned.1.call-start = ((), (), s32[]{:S(2)}) async-start(), calls=%async_computation.4 | async-start | bytes 3727360 | tf_op jit(solution)/shard_map/all_gather | solution.py:97
  893.9 203.4 %all-gather.7.cloned.1.call-start = ((), (), s32[]{:S(2)}) async-start(), calls=%async_computation.5 | async-start | bytes 4128768 | tf_op jit(solution)/shard_map/all_gather | solution.py:102
  979.8 9.3 copy-start.2
  979.8 9.3 copy-start.3
  979.8 161.9 %all-to-all-start.3 = ((bf16[8,896,256]{1,2,0:T(8,128)(2,1)}), bf16[8,896,256]{1,2,0:T(8,128)(2,1)}, u32[]{:S(2)}, u32[]{:S(2)}) async-start(bf16[8,896,256]{1,2,0:T(8,128)(2,1)} %copy.32), calls=%async_computation.3 | async-start | bytes 7340032 | tf_op jit(solution)/shard_map/all_to_all | solution.py:98
  986.3 155.3 %all-gather.9.cloned.1.call-start = ((), (), s32[]{:S(2)}) async-start(), calls=%async_computation.6 | async-start | bytes 1179648 | tf_op jit(solution)/shard_map/all_gather | solution.py:100
Sparse Core Ops, SparseCore 0:
  182.9 554.3 all-reduce.2
  894.0 79.4 all-gather.4
  975.8 121.4 all-gather.6
  1099.3 42.2 all-gather.8
where the time goes:
time: 1150 us
  waiting for transfers between devices  786 us (68%)
  blocking collectives  302 us (26%)
  matrix products  21.1 us (2%)
  starting transfers between devices  17.1 us (1%)
  between operations  13.9 us (1%)
    psum x1, waiting for transfers between devices, shards(): pre_gate, pre_up, hid_grad = lax.psum((gate_part, up_part, hid_part), 'tp')  555 us
    psum x1, blocking collectives, shards(): square = lax.psum(jnp.sum(stream * stream, axis=0), 'tp')  150 us
    psum x1, blocking collectives, shards(): dots = lax.psum(jnp.sum(scaled * normed, axis=0), 'tp')  142 us
    all_gather x1, waiting for transfers between devices, shards(): lax.all_gather(w_out, 'ep', axis=0, tiled=True)  107 us
    all_gather x1, waiting for transfers between devices, shards(): full_grad = lax.all_gather(resid, 'tp', axis=0, tiled=True)  78.9 us
    all_gather x1, waiting for transfers between devices, shards(): ctx_all = lax.all_gather(ctx_local, 'ep', axis=1, tiled=True)  39.3 us
  transfers between devices with their start and end apart: 7, of which 6 were waited for; matrix products, arithmetic and copies ran while one was open for 2% of the time, Pallas kernels for 0%

commit v1 on v0

--- a/solution.py
+++ b/solution.py
@@ -99,7 +99,12 @@
     ctx_local = context[0]
     ctx_all = lax.all_gather(ctx_local, "ep", axis=1, tiled=True)
     weight_sum = contract_cols(grad_block, ctx_all)
-    ctx_total = contract_rows(lax.all_gather(w_out, "ep", axis=0, tiled=True), full_grad)
+    ctx_total = contract_rows(
+        jnp.concatenate(
+            lax.all_to_all(jnp.stack([w_out] * lax.axis_size("ep")), "ep", 0, 0), axis=0
+        ),
+        full_grad,
+    )
     return (
         resid[None],
         ctx_total.astype(jnp.bfloat16)[None],

time: 1150 us -> 1060 us (0.922)
  the two profiles are of different devices: /device:TPU:2 before, /device:TPU:1 now
where the time goes in v1:
time: 1060 us
  waiting for transfers between devices  697 us (66%)
  blocking collectives  296 us (28%)
  matrix products  21.1 us (2%)
  starting transfers between devices  18.6 us (2%)
  between operations  15.6 us (1%)
    psum x1, waiting for transfers between devices, shards(): pre_gate, pre_up, hid_grad = lax.psum((gate_part, up_part, hid_part), 'tp')  561 us
    psum x1, blocking collectives, shards(): square = lax.psum(jnp.sum(stream * stream, axis=0), 'tp')  146 us
    psum x1, blocking collectives, shards(): dots = lax.psum(jnp.sum(scaled * normed, axis=0), 'tp')  141 us
    all_gather x1, waiting for transfers between devices, shards(): full_grad = lax.all_gather(resid, 'tp', axis=0, tiled=True)  76.3 us
    all_gather x1, waiting for transfers between devices, shards(): ctx_all = lax.all_gather(ctx_local, 'ep', axis=1, tiled=True)  48.1 us
  transfers between devices with their start and end apart: 7, of which 6 were waited for; matrix products, arithmetic and copies ran while one was open for 2% of the time, Pallas kernels for 0%

profile of v1, /device:TPU:1, one launch (start us, length us, event | category | flops | bytes accessed | tf_op | source)
XLA Modules:
  0.0 1062.5 jit_solution(11103021335114148634)
XLA Ops:
  8.0 0.9 fusion.32
  8.9 145.8 %psum.35 = f32[256]{0:T(256)S(1)} all-reduce(f32[256]{0:T(256)S(1)} %fusion.32), channel_id=1, replica_groups=mesh['tp'=64,'ep'=8] {'tp'}, use_global_device_ids=true, to_apply=%region_1.0 | all-reduce | flops 256 | bytes 2048 | tf_op jit(solution)/shard_map/psum | solution.py:50
  154.7 0.7 iota_compare_fusion.1
  155.5 1.6 fusion.9
  157.1 4.9 all-to-all-start.1
  162.1 1.6 fusion.11
  163.7 3.4 all-to-all-done.1
  167.1 3.3 all-to-all-start
  170.5 1.0 fusion.16
  171.6 2.1 fusion.19
  173.7 1.8 all-to-all-done
  175.5 2.0 fusion.21
  177.6 560.9 %all-reduce.3.cloned.1.call-done = (f32[64,2048]{1,0:T(8,128)}, f32[64,2048]{1,0:T(8,128)}, f32[64,2048]{1,0:T(8,128)}) async-done(((f32[64,2048]{1,0:T(8,128)}, f32[64,2048]{1,0:T(8,128)}, f32[64,2048]{1,0:T(8,128)}), (f32[64,2048]{1,0:T(8,128)}, f32[64,2048]{1,0:T(8,128)}, f32[64,2048]{1,0:T(8,128)})) %all-reduce.3.cloned.1.call-update) | async-done | bytes 1572880 | tf_op jit(solution)/shard_map/psum | solution.py:78
  738.5 1.6 multiply_convert_fusion.1
  741.2 0.7 reduce
  742.1 9.0 all_to_all.72
  751.5 140.7 %psum.39 = f32[256]{0:T(256)S(1)} all-reduce(f32[256]{0:T(256)S(1)} %get-tuple-element.35), channel_id=1, replica_groups=mesh['tp'=64,'ep'=8] {'tp'}, use_global_device_ids=true, to_apply=%region_6.0 | all-reduce | flops 256 | bytes 2048 | tf_op jit(solution)/shard_map/psum | solution.py:93
  892.2 0.7 fusion.31
  892.8 2.1 stack.2
  895.0 4.5 all-to-all-start.3
  899.5 76.3 %all-gather.4.cloned.1.call-done = bf16[7168,256]{1,0:T(8,128)(2,1)} async-done(((bf16[112,256]{1,0:T(8,128)(2,1)}), bf16[7168,256]{1,0:T(8,128)(2,1)}) %all-gather.4.cloned.1.call-update) | async-done | bytes 3670032 | tf_op jit(solution)/shard_map/all_gather | solution.py:97
  975.7 6.2 copy.32
  982.0 5.7 all-to-all-start.4
  987.7 0.5 all-gather.6.cloned.1.call-update
  988.3 1.1 fusion
  989.3 1.1 fusion.1
  990.4 1.1 fusion.2
  991.5 4.3 fusion.3
  995.8 0.8 copy.33
  996.6 48.1 %all-gather.6.cloned.1.call-done = bf16[1,256,2048]{2,1,0:T(8,128)(2,1)} async-done(((bf16[1,256,256]{2,1,0:T(8,128)(2,1)}), bf16[1,256,2048]{2,1,0:T(8,128)(2,1)}) %all-gather.6.cloned.1.call-update) | async-done | bytes 1048592 | tf_op jit(solution)/shard_map/all_gather | solution.py:100
  1044.7 6.2 all-to-all-done.4
  1050.8 4.3 convolution_convert_fusion.3
  (33 shorter events, 1.8 us)
Async XLA Ops:
  8.0 162.5 %copy-start = (bf16[1,112,2048]{2,1,0:T(8,128)(2,1)S(1)}, bf16[1,112,2048]{2,1,0:T(8,128)(2,1)}, u32[]{:S(2)}) copy-start(bf16[1,112,2048]{2,1,0:T(8,128)(2,1)} %param.16) | copy-start | bytes 1376260
  157.1 10.0 all-to-all-start.1
  167.1 8.3 all-to-all-start
  170.5 569.9 %copy-start.1 = (bf16[1,112,2048]{2,1,0:T(8,128)(2,1)S(1)}, bf16[1,112,2048]{2,1,0:T(8,128)(2,1)}, u32[]{:S(2)}) copy-start(bf16[1,112,2048]{2,1,0:T(8,128)(2,1)} %param.17) | copy-start | bytes 1376260
  170.5 568.0 %all-reduce.3.cloned.1.call-start = ((), (), s32[]{:S(2)}) async-start(), calls=%async_computation.7 | async-start | bytes 3145728 | tf_op jit(solution)/shard_map/psum | solution.py:78
  171.6 579.6 %copy-start.5 = (bf16[1,112,256]{2,1,0:T(8,128)(2,1)S(1)}, bf16[1,112,256]{2,1,0:T(8,128)(2,1)}, u32[]{:S(2)}) copy-start(bf16[1,112,256]{2,1,0:T(8,128)(2,1)} %param.11) | copy-start | bytes 172036
  171.6 579.6 %copy-start.7 = (s32[1,8,8]{2,1,0:T(8,128)S(1)}, s32[1,8,8]{2,1,0:T(8,128)}, u32[]{:S(2)}) copy-start(s32[1,8,8]{2,1,0:T(8,128)} %param.19) | copy-start | bytes 772
  171.6 579.6 %copy-start.8 = (f32[112]{0:T(128)S(1)}, f32[112]{0:T(128)}, u32[]{:S(2)}) copy-start(f32[112]{0:T(128)} %param.13) | copy-start | bytes 1348
  171.6 720.6 %copy-start.6 = (bf16[1,112,256]{2,1,0:T(8,128)(2,1)S(1)}, bf16[1,112,256]{2,1,0:T(8,128)(2,1)}, u32[]{:S(2)}) copy-start(bf16[1,112,256]{2,1,0:T(8,128)(2,1)} %param.12) | copy-start | bytes 172036
  173.7 719.2 %copy-start.4 = (bf16[896,256]{1,0:T(8,128)(2,1)S(1)}, bf16[896,256]{1,0:T(8,128)(2,1)}, u32[]{:S(2)}) copy-start(bf16[896,256]{1,0:T(8,128)(2,1)} %param.15) | copy-start | bytes 1376260
  177.5 798.2 %all-gather.4.cloned.1.call-start = ((), (), s32[]{:S(2)}) async-start(), calls=%async_computation.5 | async-start | bytes 3727360 | tf_op jit(solution)/shard_map/all_gather | solution.py:97
  895.0 87.0 %all-to-all-start.3 = ((bf16[8,896,256]{2,1,0:T(8,128)(2,1)}), bf16[8,896,256]{2,1,0:T(8,128)(2,1)}, u32[]{:S(2)}, u32[]{:S(2)}) async-start(bf16[8,896,256]{2,1,0:T(8,128)(2,1)} %stack.2), calls=%async_computation.3 | async-start | bytes 7340032 | tf_op jit(solution)/shard_map/all_to_all | solution.py:104
  982.0 8.4 copy-start.2
  982.0 8.4 copy-start.3
  982.0 68.9 %all-to-all-start.4 = ((bf16[8,896,256]{1,2,0:T(8,128)(2,1)}), bf16[8,896,256]{1,2,0:T(8,128)(2,1)}, u32[]{:S(2)}, u32[]{:S(2)}) async-start(bf16[8,896,256]{1,2,0:T(8,128)(2,1)} %copy.32), calls=%async_computation.4 | async-start | bytes 7340032 | tf_op jit(solution)/shard_map/all_to_all | solution.py:98
  987.7 57.0 %all-gather.6.cloned.1.call-start = ((), (), s32[]{:S(2)}) async-start(), calls=%async_computation.6 | async-start | bytes 1179648 | tf_op jit(solution)/shard_map/all_gather | solution.py:100
Sparse Core Ops, SparseCore 0:
  177.7 560.7 all-reduce.2
  893.0 82.7 all-gather.3
Sparse Core Ops, SparseCore 1:
  990.3 54.3 all-gather.5
